TPU v7x, 512 devices: a whole 4x4x16 slice. The times are simulated.
512 devices in a mesh: grp: 16 (over y, x), tok: 32 (over z, core).
Axes of the slice: x: 4, y: 4, z: 16, core: 2. Of those that a mesh axis runs over, the one named last changes fastest.
Arguments:
- hidden_in: bfloat16 [16, 4096, 1024], P('grp', 'tok'), may hold values from -6 to 6
- lengths: int32 [16, 3], P('grp'), may hold values from 1 to 3072, 4096 in all within a row
- prefix_cache: bfloat16 [16, 512, 512], P('grp', 'tok'), may hold values from -2600 to 2600
- routes: int32 [16, 4096, 8], P('grp', 'tok'), may hold values from 0 to 31, all different within a row; in each aligned block of 128 rows (0 to 127, 128 to 255, ..., all dimensions but the last counted through in order) at most 40 rows name the same one
- gates: float32 [16, 4096, 8], P('grp', 'tok'), may hold values from 0.05 to 0.4
- attn_gain: float32 [1024], replicated, may hold values from 0.1 to 1.9
- w_qkv: bfloat16 [1024, 1024], P('grp', 'tok'), may hold values from -0.75 to 0.75
- w_out: bfloat16 [512, 1024], P('grp', 'tok'), may hold values from -0.25 to 0.25
- moe_gain: float32 [1024], replicated, may hold values from 0.1 to 1.9
- expert_gate_up: bfloat16 [32, 1024, 1024], P('tok', 'grp'), may hold values from -0.1875 to 0.1875
- expert_down: bfloat16 [32, 512, 1024], P('tok', 'grp'), may hold values from -0.25 to 0.25
Outputs:
- hidden_out: bfloat16 [16, 4096, 1024], P('grp', 'tok')
- suffix_cache: bfloat16 [16, 4096, 512], P('grp', 'tok')
Inputs may be any that keep to these rules, and one draw needn't show every extreme that they name: Each group's 3 lengths sum to 4096; no request is longer than 3072 tokens, and some request of every draw has exactly 3072. `routes`: each token names 8 different experts. Among the 128 tokens of one device no expert is named more than 40 times, a bound that some block reaches.
All inputs are finite; a program needn't handle non-finite values.
Results may differ from a plain program's by a relative error of at most 0.02.
Values may be sent and summed in bfloat16 or wider, within the bound.
A program may use at most 128 MiB of HBM per device.

v0:
```python
import jax
import jax.numpy as jnp
from jax import lax
from jax.sharding import PartitionSpec as P

HEADS = 8
KV_HEADS = 4
HEAD_DIM = 64
FF = 512
EXPERTS = 32
TOP = 8
CAP = 40
epsilon = 1e-05
score_scale = 0.015625
rope_base = 10000.0
big_negative = -1e30


def rms_scale(values, gain):
    values = values.astype(jnp.float32)
    mean_square = jnp.mean(values * values, axis=-1, keepdims=True)
    return values * lax.rsqrt(mean_square + epsilon) * gain


def request_layout(group_lengths, token_index):
    ends = jnp.cumsum(group_lengths)
    starts = ends - group_lengths
    segment = jnp.sum((token_index[:, None] >= ends[None, :]).astype(jnp.int32), axis=1)
    match = segment[:, None] == jnp.arange(group_lengths.shape[0], dtype=jnp.int32)[None, :]
    offset = token_index - jnp.sum(jnp.where(match, starts[None, :], 0), axis=1)
    return (segment, offset)


def rotate(values, position):
    half_width = values.shape[-1] // 2
    frequency = rope_base ** (-jnp.arange(half_width, dtype=jnp.float32) * 2.0 / values.shape[-1])
    angle = position.astype(jnp.float32)[:, None] * frequency[None, :]
    cosine = jnp.cos(angle)[:, None, :]
    sine = jnp.sin(angle)[:, None, :]
    first = values[..., :half_width]
    second = values[..., half_width:]
    return jnp.concatenate(
        [first * cosine - second * sine, second * cosine + first * sine], axis=-1
    )


def gather_small(blocks):
    flat = jnp.concatenate([b.reshape(-1) for b in blocks])
    gathered = lax.all_gather(flat[None], "tok", axis=0, tiled=True)
    pieces, start = ([], 0)
    for b in blocks:
        size = b.size
        pieces.append(gathered[:, start : start + size].reshape((-1,) + b.shape[1:]))
        start += size
    return pieces


def gather_rows(by_columns):
    return lax.all_gather(by_columns[None], "grp", axis=0, tiled=True)


def attend(carry, grouped, keys_values, allowed):
    best, total, mixed = carry
    key_count = keys_values.shape[0]
    key_width = KV_HEADS * HEAD_DIM
    key_heads = keys_values[:, :key_width].reshape(key_count, KV_HEADS, HEAD_DIM).transpose(1, 0, 2)
    value_heads = (
        keys_values[:, key_width:].reshape(key_count, KV_HEADS, HEAD_DIM).transpose(1, 0, 2)
    )
    scores = (
        jnp.einsum("kqd,knd->kqn", grouped, key_heads, preferred_element_type=jnp.float32)
        * score_scale
    )
    if allowed is not None:
        row_count = grouped.shape[1]
        share = row_count // allowed.shape[0]
        mask = jnp.broadcast_to(allowed[:, None, :], (allowed.shape[0], share, key_count)).reshape(
            row_count, key_count
        )
        scores = jnp.where(mask[None], scores, big_negative)
    new_best = jnp.maximum(best, jnp.max(scores, axis=-1))
    factor = jnp.exp(best - new_best)
    probs = jnp.exp(scores - new_best[..., None])
    total = total * factor + jnp.sum(probs, axis=-1)
    mixed = mixed * factor[..., None] + jnp.einsum(
        "kqn,knd->kqd", probs.astype(jnp.bfloat16), value_heads, preferred_element_type=jnp.float32
    )
    return (new_best, total, mixed)


def local(
    hidden_in,
    lengths,
    prefix_cache,
    routes,
    gates,
    attn_gain,
    w_qkv,
    w_out,
    moe_gain,
    expert_gate_up,
    expert_down,
):
    tokens_here = hidden_in[0]
    tok_count = tokens_here.shape[0]
    axis_count = lax.axis_size("tok")
    device_place = lax.axis_index("tok")
    group_lengths = lengths[0]
    token_index = device_place * tok_count + jnp.arange(tok_count, dtype=jnp.int32)
    segment, offset = request_layout(group_lengths, token_index)
    position = prefix_cache.shape[1] * axis_count + offset
    query_width = HEADS * HEAD_DIM
    key_width = KV_HEADS * HEAD_DIM
    group_share = HEADS // KV_HEADS
    normed = rms_scale(tokens_here, attn_gain).astype(jnp.bfloat16)
    qkv_columns, out_columns, prefix_all = gather_small([w_qkv.T, w_out.T, prefix_cache[0]])
    qkv_weight = gather_rows(qkv_columns)
    projected = jnp.einsum(
        "ngr,gcr->nc",
        normed.reshape(tok_count, qkv_weight.shape[0], qkv_weight.shape[2]),
        qkv_weight,
        preferred_element_type=jnp.float32,
    )
    query = rotate(projected[:, :query_width].reshape(tok_count, HEADS, HEAD_DIM), position).astype(
        jnp.bfloat16
    )
    keys_new = rotate(
        projected[:, query_width : query_width + key_width].reshape(tok_count, KV_HEADS, HEAD_DIM),
        position,
    ).astype(jnp.bfloat16)
    values_new = projected[:, query_width + key_width :].astype(jnp.bfloat16)
    suffix_cache = jnp.concatenate([keys_new.reshape(tok_count, key_width), values_new], axis=1)
    row_count = tok_count * group_share
    grouped = (
        query.reshape(tok_count, KV_HEADS, group_share, HEAD_DIM)
        .transpose(1, 0, 2, 3)
        .reshape(KV_HEADS, row_count, HEAD_DIM)
    )
    start_carry = (
        jnp.full((KV_HEADS, row_count), big_negative, jnp.float32),
        jnp.zeros((KV_HEADS, row_count), jnp.float32),
        jnp.zeros((KV_HEADS, row_count, HEAD_DIM), jnp.float32),
    )
    carry = attend(start_carry, grouped, prefix_all, None)
    piece = lax.all_gather(suffix_cache, "tok", axis=0, tiled=True)
    key_index = jnp.arange(piece.shape[0], dtype=jnp.int32)
    key_segment, key_offset = request_layout(group_lengths, key_index)
    earlier = key_index[None, :] <= token_index[:, None]
    same_request = key_segment[None, :] == segment[:, None]
    carry = attend(carry, grouped, piece, earlier & same_request & (key_index[None, :] >= 0))
    best, total, mixed = carry
    attended = (mixed / total[..., None]).reshape(KV_HEADS, tok_count, group_share, HEAD_DIM)
    attended = attended.transpose(1, 0, 2, 3).reshape(tok_count, query_width).astype(jnp.bfloat16)
    out_weight = gather_rows(out_columns)
    projected_out = jnp.einsum(
        "ngr,gcr->nc",
        attended.reshape(tok_count, out_weight.shape[0], out_weight.shape[2]),
        out_weight,
        preferred_element_type=jnp.float32,
    )
    after_attention = tokens_here.astype(jnp.float32) + projected_out
    moe_in = rms_scale(after_attention, moe_gain).astype(jnp.bfloat16)
    model_width = moe_in.shape[1]
    flat_routes = routes[0].reshape(-1)
    onehot = (flat_routes[:, None] == jnp.arange(EXPERTS, dtype=jnp.int32)[None, :]).astype(
        jnp.int32
    )
    slot_rank = jnp.sum(jnp.cumsum(onehot, axis=0) * onehot, axis=1) - 1
    slot_index = flat_routes * CAP + slot_rank
    source_token = jnp.arange(flat_routes.shape[0], dtype=jnp.int32) // TOP
    outgoing = (
        jnp.zeros((EXPERTS * CAP, model_width), jnp.bfloat16)
        .at[slot_index]
        .set(moe_in[source_token])
    )
    arrived = lax.all_to_all(
        outgoing.reshape(EXPERTS, CAP, model_width), "tok", split_axis=0, concat_axis=0, tiled=True
    ).reshape(1, EXPERTS * CAP, model_width)
    sliced = arrived
    hidden_pair = jnp.einsum(
        "erd,edf->erf",
        sliced,
        lax.all_gather(expert_gate_up, "grp", axis=1, tiled=True),
        preferred_element_type=jnp.float32,
    )
    activated = (jax.nn.silu(hidden_pair[..., :FF]) * hidden_pair[..., FF:]).astype(jnp.bfloat16)
    sliced = activated
    expert_result = jnp.einsum(
        "erf,efd->erd",
        sliced,
        lax.all_gather(expert_down, "grp", axis=1, tiled=True),
        preferred_element_type=jnp.float32,
    ).astype(jnp.bfloat16)
    returned = lax.all_to_all(
        expert_result.reshape(EXPERTS, CAP, model_width),
        "tok",
        split_axis=0,
        concat_axis=0,
        tiled=True,
    ).reshape(EXPERTS * CAP, -1)
    weighted = returned[slot_index].astype(jnp.float32) * gates[0].reshape(-1)[:, None]
    moe_out = jnp.sum(weighted.reshape(tok_count, TOP, -1), axis=1)
    hidden_out = (after_attention + moe_out).astype(jnp.bfloat16)
    return (hidden_out[None], suffix_cache[None])


def solution(mesh):
    return jax.shard_map(
        local,
        mesh=mesh,
        in_specs=(
            P("grp", "tok", None),
            P("grp", None),
            P("grp", "tok", None),
            P("grp", "tok", None),
            P("grp", "tok", None),
            P(),
            P("grp", "tok"),
            P("grp", "tok"),
            P(),
            P("tok", "grp", None),
            P("tok", "grp", None),
        ),
        out_specs=(P("grp", "tok", None), P("grp", "tok", None)),
        check_vma=False,
    )
```

profile of v0, /device:TPU:32, one launch (start us, length us, event | category | flops | bytes accessed | tf_op | source)
XLA Modules:
  0.0 550.5 jit_solution(17672893901105111063)
XLA Ops:
  9.7 36.1 %all-gather = bf16[360448]{0:T(1024)(128)(2,1)S(1)} all-gather(bf16[11264]{0:T(1024)(128)(2,1)S(1)} %pad_maximum_fusion.3), channel_id=2, replica_groups=mesh['grp'=16,'tok'=32] {'tok'}, dimensions={0}, use_global_device_ids=true | all-gather | bytes 743424 | tf_op jit(solution)/shard_map/all_gather | solution.py:49
  48.1 57.2 %all-gather.7.cloned.1.call-done = bf16[16,1024,64]{1,2,0:T(8,128)(2,1)} async-done(((bf16[1,1024,64]{1,2,0:T(8,128)(2,1)}), bf16[16,1024,64]{1,2,0:T(8,128)(2,1)}) %all-gather.7.cloned.1.call-update) | async-done | bytes 2097168 | tf_op jit(solution)/shard_map/all_gather | solution.py:59
  105.3 2.3 convolution_bitcast_fusion.2
  112.4 2.4 broadcast_in_dim.44
  114.8 2.6 broadcast_in_dim.49
  120.0 9.0 %reduce-window.11 = s32[32,8,128]{2,1,0:T(8,128)S(1)} reduce-window(s32[32,8,128]{2,1,0:T(8,128)S(1)} %fusion.32, s32[]{:T(128)} %constant.34.clone.1), window={size=1x1x128 pad=0_0x0_0x127_0}, to_apply=%region_9.10 | reduce-window | flops 4161536 | bytes 262148 | tf_op jit(solution)/shard_map/reduce-window.1
  132.6 50.5 %all-gather.9.cloned.1.call-done = bf16[4096,512]{1,0:T(8,128)(2,1)} async-done(((bf16[128,512]{1,0:T(8,128)(2,1)}), bf16[4096,512]{1,0:T(8,128)(2,1)}) %all-gather.9.cloned.1.call-update) | async-done | bytes 4194320 | tf_op jit(solution)/shard_map/all_gather | solution.py:145
  183.1 3.8 fusion.40
  186.9 2.9 copy.101
  189.8 2.9 copy.99
  192.8 3.5 fusion
  196.3 4.6 fusion.1
  203.2 11.2 %fusion.3 = f32[4,256,64]{1,2,0:T(8,128)} fusion(bf16[4,4096,64]{1,2,0:T(8,128)(2,1)} %bitcast.104, f32[4,256,4096]{2,1,0:T(8,128)} %copy-done, f32[4,256]{1,0:T(4,128)S(1)} %get-tuple-element.15, pred[256,4096]{1,0:T(8,128)(4,1)S(1)} %broadcast_in_dim.49), kind=kOutput, calls=%fused_computation.8 | convolution fusion | flops 553648128 | bytes 20189184 | tf_op jit(solution)/shard_map/kqn,knd->kqd/dot_general | solution.py:85
  216.4 24.7 %all-gather.11.cloned.1.call-done = bf16[16,1024,32]{1,2,0:T(8,128)(2,1)} async-done(((bf16[1,1024,32]{1,2,0:T(8,128)(2,1)}), bf16[16,1024,32]{1,2,0:T(8,128)(2,1)}) %all-gather.11.cloned.1.call-update) | async-done | bytes 1048592 | tf_op jit(solution)/shard_map/all_gather | solution.py:59
  242.8 14.7 %scatter_custom_fusion = bf16[1280,1024]{1,0:T(8,128)(2,1)} fusion(s32[1024]{0:T(1024)S(1)} %bitcast.118, bf16[128,1024]{1,0:T(8,128)(2,1)S(1)} %multiply_convert_fusion, s32[1024]{0:T(1024)S(1)} %broadcast_clamp_fusion.1, bf16[]{:T(256)} %constant.67.clone.1), kind=kCustom, calls=%fused_computation.17 | custom fusion | bytes 2621442 | tf_op jit(solution)/shard_map/scatter | solution.py:174
  257.6 12.8 %all-to-all-start = ((bf16[32,40,1024]{2,1,0:T(8,128)(2,1)}), bf16[32,40,1024]{2,1,0:T(8,128)(2,1)S(1)}, u32[]{:S(2)}, u32[]{:S(2)}) async-start(bf16[32,40,1024]{2,1,0:T(8,128)(2,1)} %bitcast.34), calls=%async_computation | async-start | bytes 5242880 | tf_op jit(solution)/shard_map/all_to_all | solution.py:176
  271.6 61.4 %all-gather.13.cloned.1.call-done = bf16[1,1024,1024]{2,1,0:T(8,128)(2,1)} async-done(((bf16[1,64,1024]{2,1,0:T(8,128)(2,1)}), bf16[1,1024,1024]{2,1,0:T(8,128)(2,1)}) %all-gather.13.cloned.1.call-update) | async-done | bytes 2097168 | tf_op jit(solution)/shard_map/all_gather | solution.py:183
  332.9 60.2 %all-to-all-done = bf16[32,40,1024]{2,1,0:T(8,128)(2,1)S(1)} async-done(((bf16[32,40,1024]{2,1,0:T(8,128)(2,1)}), bf16[32,40,1024]{2,1,0:T(8,128)(2,1)S(1)}, u32[]{:S(2)}, u32[]{:S(2)}) %all-to-all-start) | async-done | bytes 2621472 | tf_op jit(solution)/shard_map/all_to_all | solution.py:176
  393.1 6.2 %convolution_bitcast_fusion = f32[1,1280,1024]{2,1,0:T(8,128)} fusion(bf16[1280,1024]{1,0:T(8,128)(2,1)S(1)} %bitcast.102, bf16[1,1024,1024]{2,1,0:T(8,128)(2,1)} %all-gather.13.cloned.1.call-done), kind=kOutput, calls=%fused_computation.10 | convolution fusion | flops 2684354560 | bytes 9961472 | tf_op jit(solution)/shard_map/erd,edf->erf/dot_general | solution.py:180
  399.3 5.9 %convolution_convert_fusion = bf16[1280,1024]{1,0:T(8,128)(2,1)} fusion(f32[1,1280,1024]{2,1,0:T(8,128)} %convolution_bitcast_fusion, bf16[1,512,1024]{2,1,0:T(8,128)(2,1)} %all-gather.15.cloned.1.call-done), kind=kOutput, calls=%fused_computation.13 | convolution fusion | flops 1347420160 | bytes 8912896 | tf_op jit(solution)/shard_map/erf,efd->erd/dot_general | solution.py:188
  405.2 6.9 %all-to-all-start.1 = ((bf16[32,40,1024]{2,1,0:T(8,128)(2,1)}), bf16[32,40,1024]{2,1,0:T(8,128)(2,1)S(1)}, u32[]{:S(2)}, u32[]{:S(2)}) async-start(bf16[32,40,1024]{2,1,0:T(8,128)(2,1)} %bitcast.103), calls=%async_computation.1 | async-start | bytes 5242880 | tf_op jit(solution)/shard_map/all_to_all | solution.py:194
  412.3 122.6 %all-to-all-done.1 = bf16[32,40,1024]{2,1,0:T(8,128)(2,1)S(1)} async-done(((bf16[32,40,1024]{2,1,0:T(8,128)(2,1)}), bf16[32,40,1024]{2,1,0:T(8,128)(2,1)S(1)}, u32[]{:S(2)}, u32[]{:S(2)}) %all-to-all-start.1) | async-done | bytes 2621472 | tf_op jit(solution)/shard_map/all_to_all | solution.py:194
  534.9 5.4 gather_fusion
  540.2 2.9 fusion.6
  (109 shorter events, 23.4 us)
Async XLA Ops:
  7.2 40.0 %copy-start.2 = (bf16[1,128,1024]{2,1,0:T(8,128)(2,1)S(1)}, bf16[1,128,1024]{2,1,0:T(8,128)(2,1)}, u32[]{:S(2)}) copy-start(bf16[1,128,1024]{2,1,0:T(8,128)(2,1)} %param.11) | copy-start | bytes 786436
  7.2 40.1 %copy-start.8 = (f32[1024]{0:T(1024)S(1)}, f32[1024]{0:T(1024)}, u32[]{:S(2)}) copy-start(f32[1024]{0:T(1024)} %param.16) | copy-start | bytes 12292
  7.2 40.2 %copy-start.10 = (s32[1,3]{1,0:T(1,128)S(1)}, s32[1,3]{1,0:T(1,128)}, u32[]{:S(2)}) copy-start(s32[1,3]{1,0:T(1,128)} %param.12) | copy-start | bytes 40
  7.2 98.1 %all-gather.7.cloned.1.call-start = ((), (), s32[]{:S(2)}) async-start(), calls=%async_computation.2 | async-start | bytes 2228224 | tf_op jit(solution)/shard_map/all_gather | solution.py:59
  47.1 136.0 %all-gather.9.cloned.1.call-start = ((), (), s32[]{:S(2)}) async-start(), calls=%async_computation.3 | async-start | bytes 4325376 | tf_op jit(solution)/shard_map/all_gather | solution.py:145
  105.3 6.3 %copy-start.6 = (s32[1,128,8]{1,2,0:T(8,128)S(1)}, s32[1,128,8]{1,2,0:T(8,128)}, u32[]{:S(2)}) copy-start(s32[1,128,8]{1,2,0:T(8,128)} %param.14) | copy-start | bytes 12292
  107.6 0.8 copy-start.4
  109.4 131.6 %all-gather.11.cloned.1.call-start = ((), (), s32[]{:S(2)}) async-start(), calls=%async_computation.4 | async-start | bytes 1114112 | tf_op jit(solution)/shard_map/all_gather | solution.py:59
  117.4 12.2 %slice-start = ((f32[128,1024]{1,0:T(8,128)}), f32[128,512]{1,0:T(8,128)S(1)}, s32[]{:S(2)}) async-start(f32[128,1024]{1,0:T(8,128)} %copy-done.4), calls=%async_computation.7 | async-start | bytes 524288 | tf_op jit(solution)/shard_map/slice | solution.py:124
  196.2 6.4 %copy-start = (f32[4,256,4096]{2,1,0:T(8,128)}, f32[4,256,4096]{2,1,0:T(8,128)S(1)}, u32[]{:S(2)}) copy-start(f32[4,256,4096]{2,1,0:T(8,128)S(1)} %get-tuple-element.22) | copy-start | bytes 50331652
  196.3 6.4 %copy-start.1 = (f32[4,256,512]{2,1,0:T(8,128)S(1)}, f32[4,256,512]{2,1,0:T(8,128)}, u32[]{:S(2)}) copy-start(f32[4,256,512]{2,1,0:T(8,128)} %get-tuple-element.20) | copy-start | bytes 6291460
  203.2 11.2 %copy-start.5 = (bf16[512,256]{0,1:T(8,128)(2,1)S(1)}, bf16[512,256]{0,1:T(8,128)(2,1)}, u32[]{:S(2)}) copy-start(bf16[512,256]{0,1:T(8,128)(2,1)} %copy.96) | copy-start | bytes 786436
  214.5 26.6 %copy-start.3 = (bf16[1,128,1024]{2,1,0:T(8,128)(2,1)S(1)}, bf16[1,128,1024]{2,1,0:T(8,128)(2,1)}, u32[]{:S(2)}) copy-start(bf16[1,128,1024]{2,1,0:T(8,128)(2,1)} %param.11) | copy-start | bytes 786436
  214.5 28.3 %copy-start.7 = (f32[1024]{0:T(1024)S(1)}, f32[1024]{0:T(1024)}, u32[]{:S(2)}) copy-start(f32[1024]{0:T(1024)} %param.19) | copy-start | bytes 12292
  257.6 135.5 %all-to-all-start = ((bf16[32,40,1024]{2,1,0:T(8,128)(2,1)}), bf16[32,40,1024]{2,1,0:T(8,128)(2,1)S(1)}, u32[]{:S(2)}, u32[]{:S(2)}) async-start(bf16[32,40,1024]{2,1,0:T(8,128)(2,1)} %bitcast.34), calls=%async_computation | async-start | bytes 5242880 | tf_op jit(solution)/shard_map/all_to_all | solution.py:176
  270.4 62.5 %all-gather.13.cloned.1.call-start = ((), (), s32[]{:S(2)}) async-start(), calls=%async_computation.5 | async-start | bytes 2228224 | tf_op jit(solution)/shard_map/all_gather | solution.py:183
  271.0 128.3 %all-gather.15.cloned.1.call-start = ((), (), s32[]{:S(2)}) async-start(), calls=%async_computation.6 | async-start | bytes 1114112 | tf_op jit(solution)/shard_map/all_gather | solution.py:191
  405.2 6.9 %copy-start.9 = (f32[1,128,8]{1,2,0:T(8,128)S(1)}, f32[1,128,8]{1,2,0:T(8,128)}, u32[]{:S(2)}) copy-start(f32[1,128,8]{1,2,0:T(8,128)} %param.15) | copy-start | bytes 12292
  405.2 129.7 %all-to-all-start.1 = ((bf16[32,40,1024]{2,1,0:T(8,128)(2,1)}), bf16[32,40,1024]{2,1,0:T(8,128)(2,1)S(1)}, u32[]{:S(2)}, u32[]{:S(2)}) async-start(bf16[32,40,1024]{2,1,0:T(8,128)(2,1)} %bitcast.103), calls=%async_computation.1 | async-start | bytes 5242880 | tf_op jit(solution)/shard_map/all_to_all | solution.py:194
Sparse Core Ops, SparseCore 0:
  47.2 58.0 all-gather.6
  109.5 73.5 all-gather.8
  186.1 54.9 all-gather.10
  273.9 58.9 all-gather.12
  335.8 57.4 all-gather.14
where the time goes:
time: 551 us; the launch traced here: 550 us
  waiting for transfers between devices  378 us (69%)
  local copies, waits for them, and re-layouts  47.2 us (9%)
  blocking collectives  36.1 us (7%)
  matrix products  34.1 us (6%)
  other arithmetic  21 us (4%)
  starting transfers between devices  20.1 us (4%)
  between operations  14.3 us (3%)
    all_to_all x1, waiting for transfers between devices, local(): lax.all_to_all(expert_result.reshape(EXPERTS, CAP, model_width), 'tok', s...  123 us
    all_gather x2, waiting for transfers between devices, gather_rows(): return lax.all_gather(by_columns[None], 'grp', axis=0, tiled=True)  81.9 us
    all_gather x1, waiting for transfers between devices, local(): lax.all_gather(expert_gate_up, 'grp', axis=1, tiled=True)  61.4 us
    all_to_all x1, waiting for transfers between devices, local(): lax.all_to_all(outgoing.reshape(EXPERTS, CAP, model_width), 'tok', split_...  60.2 us
    all_gather x1, waiting for transfers between devices, local(): piece = lax.all_gather(suffix_cache, 'tok', axis=0, tiled=True)  50.5 us
    all_gather x1, blocking collectives, gather_small(): gathered = lax.all_gather(flat[None], 'tok', axis=0, tiled=True)  36.1 us
    scatter x1, local copies, waits for them, and re-layouts, local(): outgoing = jnp.zeros((EXPERTS * CAP, model_width), jnp.bfloat16).at[slot_...  14.7 us
    dot_general x2, matrix products, attend(): jnp.einsum('kqn,knd->kqd', probs.astype(jnp.bfloat16), value_heads, prefe...  12.8 us
  transfers between devices with their start and end apart: 7, of which 6 were waited for; matrix products, arithmetic and copies ran while one was open for 11% of the time, Pallas kernels for 0%

commit v1 on v0

--- a/solution.py
+++ b/solution.py
@@ -180,7 +180,15 @@
     hidden_pair = jnp.einsum(
         "erd,edf->erf",
         sliced,
-        lax.all_gather(expert_gate_up, "grp", axis=1, tiled=True),
+        jnp.concatenate(
+            jax.lax.all_to_all(
+                jnp.stack([expert_gate_up for _ in range(jax.lax.axis_size("grp"))]),
+                axis_name="grp",
+                split_axis=0,
+                concat_axis=0,
+            ),
+            axis=1,
+        ),
         preferred_element_type=jnp.float32,
     )
     activated = (jax.nn.silu(hidden_pair[..., :FF]) * hidden_pair[..., FF:]).astype(jnp.bfloat16)

time: 551 us -> 548 us (level)
  waiting for transfers between devices: 378 us -> 371 us
    all_to_all x1, waiting for transfers between devices: 60.2 us -> 122 us  [local(): lax.all_to_all(outgoing.reshape(EXPERTS, CAP, model_width), 'tok', split_...]
    all_gather x1 -> x0, waiting for transfers between devices: 61.4 us -> none  [local(): lax.all_gather(expert_gate_up, 'grp', axis=1, tiled=True)]
    all_gather x1, waiting for transfers between devices: 50.5 us -> 43.7 us  [local(): piece = lax.all_gather(suffix_cache, 'tok', axis=0, tiled=True)]
  transfers between devices with their start and end apart: 7 -> 7, of which waited for: 6 -> 5; matrix products, arithmetic and copies ran while one was open for 11% -> 15% of each run, Pallas kernels for 0% -> 0%
where the time goes in v1:
time: 548 us; the launch traced here: 547 us
  waiting for transfers between devices  371 us (68%)
  local copies, waits for them, and re-layouts  48.9 us (9%)
  blocking collectives  36.1 us (7%)
  matrix products  34.1 us (6%)
  starting transfers between devices  22.3 us (4%)
  other arithmetic  21 us (4%)
  between operations  14.2 us (3%)
    all_to_all x1, waiting for transfers between devices, local(): lax.all_to_all(expert_result.reshape(EXPERTS, CAP, model_width), 'tok', s...  122 us
    all_to_all x1, waiting for transfers between devices, local(): lax.all_to_all(outgoing.reshape(EXPERTS, CAP, model_width), 'tok', split_...  122 us
    all_gather x2, waiting for transfers between devices, gather_rows(): return lax.all_gather(by_columns[None], 'grp', axis=0, tiled=True)  82 us
    all_gather x1, waiting for transfers between devices, local(): piece = lax.all_gather(suffix_cache, 'tok', axis=0, tiled=True)  43.7 us
    all_gather x1, blocking collectives, gather_small(): gathered = lax.all_gather(flat[None], 'tok', axis=0, tiled=True)  36.1 us
    scatter x1, local copies, waits for them, and re-layouts, local(): outgoing = jnp.zeros((EXPERTS * CAP, model_width), jnp.bfloat16).at[slot_...  14.7 us
    dot_general x2, matrix products, attend(): jnp.einsum('kqn,knd->kqd', probs.astype(jnp.bfloat16), value_heads, prefe...  12.8 us
    all_to_all x1, starting transfers between devices, local(): lax.all_to_all(outgoing.reshape(EXPERTS, CAP, model_width), 'tok', split_...  12.8 us
  transfers between devices with their start and end apart: 7, of which 5 were waited for; matrix products, arithmetic and copies ran while one was open for 15% of the time, Pallas kernels for 0%

profile of v1, /device:TPU:32, one launch (start us, length us, event | category | flops | bytes accessed | tf_op | source)
XLA Modules:
  0.0 547.2 jit_solution(11317888462294164468)
XLA Ops:
  9.7 36.1 %all-gather = bf16[360448]{0:T(1024)(128)(2,1)S(1)} all-gather(bf16[11264]{0:T(1024)(128)(2,1)S(1)} %pad_maximum_fusion.3), channel_id=2, replica_groups=mesh['grp'=16,'tok'=32] {'tok'}, dimensions={0}, use_global_device_ids=true | all-gather | bytes 743424 | tf_op jit(solution)/shard_map/all_gather | solution.py:49
  48.1 57.2 %all-gather.6.cloned.1.call-done = bf16[16,1024,64]{1,2,0:T(8,128)(2,1)} async-done(((bf16[1,1024,64]{1,2,0:T(8,128)(2,1)}), bf16[16,1024,64]{1,2,0:T(8,128)(2,1)}) %all-gather.6.cloned.1.call-update) | async-done | bytes 2097168 | tf_op jit(solution)/shard_map/all_gather | solution.py:59
  105.3 2.3 convolution_bitcast_fusion.2
  111.0 5.1 all-to-all-start.1
  119.1 2.4 broadcast_in_dim.44
  121.5 2.6 broadcast_in_dim.49
  126.7 9.0 %reduce-window.11 = s32[32,8,128]{2,1,0:T(8,128)S(1)} reduce-window(s32[32,8,128]{2,1,0:T(8,128)S(1)} %fusion.31, s32[]{:T(128)} %constant.34.clone.1), window={size=1x1x128 pad=0_0x0_0x127_0}, to_apply=%region_9.10 | reduce-window | flops 4161536 | bytes 262148 | tf_op jit(solution)/shard_map/reduce-window.1
  139.2 43.7 %all-gather.8.cloned.1.call-done = bf16[4096,512]{1,0:T(8,128)(2,1)} async-done(((bf16[128,512]{1,0:T(8,128)(2,1)}), bf16[4096,512]{1,0:T(8,128)(2,1)}) %all-gather.8.cloned.1.call-update) | async-done | bytes 4194320 | tf_op jit(solution)/shard_map/all_gather | solution.py:145
  182.9 3.8 fusion.39
  186.8 3.0 copy.101
  189.8 2.9 copy.99
  192.7 3.5 fusion
  196.2 4.6 fusion.1
  203.2 11.2 %fusion.3 = f32[4,256,64]{1,2,0:T(8,128)} fusion(bf16[4,4096,64]{1,2,0:T(8,128)(2,1)} %bitcast.104, f32[4,256,4096]{2,1,0:T(8,128)} %copy-done, f32[4,256]{1,0:T(4,128)S(1)} %get-tuple-element.15, pred[256,4096]{1,0:T(8,128)(4,1)S(1)} %broadcast_in_dim.49), kind=kOutput, calls=%fused_computation.8 | convolution fusion | flops 553648128 | bytes 20189184 | tf_op jit(solution)/shard_map/kqn,knd->kqd/dot_general | solution.py:85
  216.3 24.8 %all-gather.10.cloned.1.call-done = bf16[16,1024,32]{1,2,0:T(8,128)(2,1)} async-done(((bf16[1,1024,32]{1,2,0:T(8,128)(2,1)}), bf16[16,1024,32]{1,2,0:T(8,128)(2,1)}) %all-gather.10.cloned.1.call-update) | async-done | bytes 1048592 | tf_op jit(solution)/shard_map/all_gather | solution.py:59
  242.9 14.7 %scatter_custom_fusion = bf16[1280,1024]{1,0:T(8,128)(2,1)} fusion(s32[1024]{0:T(1024)S(1)} %bitcast.119, bf16[128,1024]{1,0:T(8,128)(2,1)S(1)} %multiply_convert_fusion, s32[1024]{0:T(1024)S(1)} %broadcast_clamp_fusion.1, bf16[]{:T(256)} %constant.67.clone.1), kind=kCustom, calls=%fused_computation.16 | custom fusion | bytes 2621442 | tf_op jit(solution)/shard_map/scatter | solution.py:174
  257.7 12.8 %all-to-all-start = ((bf16[32,40,1024]{2,1,0:T(8,128)(2,1)}), bf16[32,40,1024]{2,1,0:T(8,128)(2,1)S(1)}, u32[]{:S(2)}, u32[]{:S(2)}) async-start(bf16[32,40,1024]{2,1,0:T(8,128)(2,1)} %bitcast.34), calls=%async_computation | async-start | bytes 5242880 | tf_op jit(solution)/shard_map/all_to_all | solution.py:176
  271.1 122.2 %all-to-all-done = bf16[32,40,1024]{2,1,0:T(8,128)(2,1)S(1)} async-done(((bf16[32,40,1024]{2,1,0:T(8,128)(2,1)}), bf16[32,40,1024]{2,1,0:T(8,128)(2,1)S(1)}, u32[]{:S(2)}, u32[]{:S(2)}) %all-to-all-start) | async-done | bytes 2621472 | tf_op jit(solution)/shard_map/all_to_all | solution.py:176
  393.2 6.2 %convolution_bitcast_fusion = f32[1,1280,1024]{2,1,0:T(8,128)} fusion(bf16[1280,1024]{1,0:T(8,128)(2,1)S(1)} %bitcast.102, bf16[1024,1024]{1,0:T(8,128)(2,1)} %bitcast.37), kind=kOutput, calls=%fused_computation.10 | convolution fusion | flops 2684354560 | bytes 9961472 | tf_op jit(solution)/shard_map/erd,edf->erf/dot_general | solution.py:180
  399.4 5.9 %convolution_convert_fusion = bf16[1280,1024]{1,0:T(8,128)(2,1)} fusion(f32[1,1280,1024]{2,1,0:T(8,128)} %convolution_bitcast_fusion, bf16[1,512,1024]{2,1,0:T(8,128)(2,1)} %all-gather.12.cloned.1.call-done), kind=kOutput, calls=%fused_computation.13 | convolution fusion | flops 1347420160 | bytes 8912896 | tf_op jit(solution)/shard_map/erf,efd->erd/dot_general | solution.py:196
  405.3 4.0 all-to-all-start.2
  409.4 122.2 %all-to-all-done.2 = bf16[32,40,1024]{2,1,0:T(8,128)(2,1)S(1)} async-done(((bf16[32,40,1024]{2,1,0:T(8,128)(2,1)}), bf16[32,40,1024]{2,1,0:T(8,128)(2,1)S(1)}, u32[]{:S(2)}, u32[]{:S(2)}) %all-to-all-start.2) | async-done | bytes 2621472 | tf_op jit(solution)/shard_map/all_to_all | solution.py:202
  531.6 5.4 gather_fusion
  537.0 2.9 fusion.6
  (111 shorter events, 24.4 us)
Async XLA Ops:
  7.2 40.0 %copy-start.2 = (bf16[1,128,1024]{2,1,0:T(8,128)(2,1)S(1)}, bf16[1,128,1024]{2,1,0:T(8,128)(2,1)}, u32[]{:S(2)}) copy-start(bf16[1,128,1024]{2,1,0:T(8,128)(2,1)} %param.11) | copy-start | bytes 786436
  7.2 40.1 %copy-start.9 = (f32[1024]{0:T(1024)S(1)}, f32[1024]{0:T(1024)}, u32[]{:S(2)}) copy-start(f32[1024]{0:T(1024)} %param.16) | copy-start | bytes 12292
  7.2 40.2 %copy-start.11 = (s32[1,3]{1,0:T(1,128)S(1)}, s32[1,3]{1,0:T(1,128)}, u32[]{:S(2)}) copy-start(s32[1,3]{1,0:T(1,128)} %param.12) | copy-start | bytes 40
  7.2 98.1 %all-gather.6.cloned.1.call-start = ((), (), s32[]{:S(2)}) async-start(), calls=%async_computation.3 | async-start | bytes 2228224 | tf_op jit(solution)/shard_map/all_gather | solution.py:59
  47.1 135.8 %all-gather.8.cloned.1.call-start = ((), (), s32[]{:S(2)}) async-start(), calls=%async_computation.4 | async-start | bytes 4325376 | tf_op jit(solution)/shard_map/all_gather | solution.py:145
  47.3 62.1 %copy-start.6 = (bf16[1,64,1024]{2,1,0:T(8,128)(2,1)S(1)}, bf16[1,64,1024]{2,1,0:T(8,128)(2,1)}, u32[]{:S(2)}) copy-start(bf16[1,64,1024]{2,1,0:T(8,128)(2,1)} %param.20) | copy-start | bytes 393220
  107.6 0.8 copy-start.4
  111.0 7.3 %copy-start.7 = (s32[1,128,8]{1,2,0:T(8,128)S(1)}, s32[1,128,8]{1,2,0:T(8,128)}, u32[]{:S(2)}) copy-start(s32[1,128,8]{1,2,0:T(8,128)} %param.14) | copy-start | bytes 12292
  111.0 146.7 %all-to-all-start.1 = ((bf16[16,1,64,1024]{3,2,1,0:T(8,128)(2,1)}), bf16[16,1,64,1024]{3,2,1,0:T(8,128)(2,1)}, u32[]{:S(2)}, u32[]{:S(2)}) async-start(bf16[16,1,64,1024]{3,2,1,0:T(8,128)(2,1)} %stack.2), calls=%async_computation.1 | async-start | bytes 4194304 | tf_op jit(solution)/shard_map/all_to_all | solution.py:184
  116.1 125.0 %all-gather.10.cloned.1.call-start = ((), (), s32[]{:S(2)}) async-start(), calls=%async_computation.5 | async-start | bytes 1114112 | tf_op jit(solution)/shard_map/all_gather | solution.py:59
  124.1 12.2 %slice-start = ((f32[128,1024]{1,0:T(8,128)}), f32[128,512]{1,0:T(8,128)S(1)}, s32[]{:S(2)}) async-start(f32[128,1024]{1,0:T(8,128)} %copy-done.4), calls=%async_computation.7 | async-start | bytes 524288 | tf_op jit(solution)/shard_map/slice | solution.py:124
  196.2 6.4 %copy-start = (f32[4,256,4096]{2,1,0:T(8,128)}, f32[4,256,4096]{2,1,0:T(8,128)S(1)}, u32[]{:S(2)}) copy-start(f32[4,256,4096]{2,1,0:T(8,128)S(1)} %get-tuple-element.22) | copy-start | bytes 50331652
  196.2 6.4 %copy-start.1 = (f32[4,256,512]{2,1,0:T(8,128)S(1)}, f32[4,256,512]{2,1,0:T(8,128)}, u32[]{:S(2)}) copy-start(f32[4,256,512]{2,1,0:T(8,128)} %get-tuple-element.20) | copy-start | bytes 6291460
  203.2 11.2 %copy-start.5 = (bf16[512,256]{0,1:T(8,128)(2,1)S(1)}, bf16[512,256]{0,1:T(8,128)(2,1)}, u32[]{:S(2)}) copy-start(bf16[512,256]{0,1:T(8,128)(2,1)} %copy.96) | copy-start | bytes 786436
  214.4 26.7 %copy-start.3 = (bf16[1,128,1024]{2,1,0:T(8,128)(2,1)S(1)}, bf16[1,128,1024]{2,1,0:T(8,128)(2,1)}, u32[]{:S(2)}) copy-start(bf16[1,128,1024]{2,1,0:T(8,128)(2,1)} %param.11) | copy-start | bytes 786436
  214.4 28.4 %copy-start.8 = (f32[1024]{0:T(1024)S(1)}, f32[1024]{0:T(1024)}, u32[]{:S(2)}) copy-start(f32[1024]{0:T(1024)} %param.19) | copy-start | bytes 12292
  257.7 135.5 %all-to-all-start = ((bf16[32,40,1024]{2,1,0:T(8,128)(2,1)}), bf16[32,40,1024]{2,1,0:T(8,128)(2,1)S(1)}, u32[]{:S(2)}, u32[]{:S(2)}) async-start(bf16[32,40,1024]{2,1,0:T(8,128)(2,1)} %bitcast.34), calls=%async_computation | async-start | bytes 5242880 | tf_op jit(solution)/shard_map/all_to_all | solution.py:176
  270.5 128.9 %all-gather.12.cloned.1.call-start = ((), (), s32[]{:S(2)}) async-start(), calls=%async_computation.6 | async-start | bytes 1114112 | tf_op jit(solution)/shard_map/all_gather | solution.py:199
  405.3 4.0 copy-start.10
  405.3 126.3 %all-to-all-start.2 = ((bf16[32,40,1024]{2,1,0:T(8,128)(2,1)}), bf16[32,40,1024]{2,1,0:T(8,128)(2,1)S(1)}, u32[]{:S(2)}, u32[]{:S(2)}) async-start(bf16[32,40,1024]{2,1,0:T(8,128)(2,1)} %bitcast.103), calls=%async_computation.2 | async-start | bytes 5242880 | tf_op jit(solution)/shard_map/all_to_all | solution.py:202
Sparse Core Ops, SparseCore 0:
  47.2 58.0 all-gather.5
  109.5 73.3 all-gather.7
  186.0 55.1 all-gather.9
  274.0 56.7 all-gather.11
